TPU v7x, 32 devices: a whole 2x2x4 slice. The times are simulated.
32 devices in a mesh: groups: 2 (over y), row: 8 (over z, x), col: 2 (over core).
Axes of the slice: x: 2, y: 2, z: 4, core: 2. Of those that a mesh axis runs over, the one named last changes fastest.
Arguments:
- inputs: bfloat16 [32, 8192], P(('groups', 'row'), 'col'), parts along dimension 0, may hold values from -6 to 6
- out_grads: bfloat16 [32, 8192], P(('groups', 'row'), 'col'), parts along dimension 0, may hold values from -6 to 6
- w_gate: bfloat16 [8192, 24576], P('col', 'row'), may hold values from -0.0625 to 0.0625
- w_up: bfloat16 [8192, 24576], P('col', 'row'), may hold values from -0.0625 to 0.0625
- w_down: bfloat16 [24576, 8192], P('row', 'col'), may hold values from -0.0390625 to 0.0390625
Outputs:
- attribution: float32 [32, 8192], P(('groups', 'row'), 'col'), parts along dimension 0
There are 2 independent parts, one for each index of `groups`. A program takes and returns all parts, laid end to end along the dimension named above; an argument that names none is the same for every part. Nothing has to cross between parts.
All inputs are finite; a program needn't handle non-finite values.
Results may differ from a plain program's by a relative error of at most 0.0029.
Values may be sent and summed in bfloat16 or wider, within the bound.
A program may use at most 192 MiB of HBM per device.

v0:
```python
import jax
import jax.numpy as jnp
from jax import lax
from jax.sharding import PartitionSpec as P


def derivatives(sums):
    gated = sums[0]
    upward = sums[1]
    backward = sums[2]
    sigma = jax.nn.sigmoid(gated)
    grad_gate = (backward * upward * sigma * (1.0 + gated * (1.0 - sigma))).astype(jnp.bfloat16)
    grad_up = (backward * gated * sigma).astype(jnp.bfloat16)
    return jnp.stack([grad_gate, grad_up])


def per_device(inputs, out_grads, w_gate, w_up, w_down):
    stacked = jnp.stack([inputs, out_grads])
    piece = lax.all_gather(stacked, "row", axis=1, tiled=True)
    gated = jnp.dot(piece[0], w_gate, preferred_element_type=jnp.float32)
    upward = jnp.dot(piece[0], w_up, preferred_element_type=jnp.float32)
    backward = lax.dot_general(
        piece[1], w_down, (((1,), (1,)), ((), ())), preferred_element_type=jnp.float32
    )
    partial_sums = jnp.stack([gated, upward, backward])
    summed = lax.psum(partial_sums, "col")
    derived = derivatives(summed)
    total = lax.dot_general(
        derived[0], w_gate, (((1,), (1,)), ((), ())), preferred_element_type=jnp.float32
    )
    grad_input = lax.psum_scatter(
        total
        + lax.dot_general(
            derived[1], w_up, (((1,), (1,)), ((), ())), preferred_element_type=jnp.float32
        ),
        "row",
        scatter_dimension=0,
        tiled=True,
    )
    return inputs.astype(jnp.float32) * grad_input


def solution(mesh):
    in_specs = (
        P(("groups", "row"), "col"),
        P(("groups", "row"), "col"),
        P("col", "row"),
        P("col", "row"),
        P("row", "col"),
    )
    out_specs = P(("groups", "row"), "col")
    return jax.shard_map(
        per_device, mesh=mesh, in_specs=in_specs, out_specs=out_specs, check_vma=False
    )
```

profile of v0, /device:TPU:0, one launch (start us, length us, event | category | flops | bytes accessed | tf_op | source)
XLA Modules:
  0.0 200.1 jit_solution(14004625171131348486)
XLA Ops:
  6.5 0.0 all-reduce.4.cloned.1.call-start
  6.5 0.8 pad_maximum_fusion.1
  7.4 32.5 %all_gather.3 = bf16[2,16,4096]{2,0,1:T(2,128)(2,1)S(1)} all-gather(bf16[2,2,4096]{2,0,1:T(2,128)(2,1)S(1)} %copy.6), channel_id=1, replica_groups=mesh['groups'=2,'row'=8,'col'=2] {'row'}, dimensions={1}, use_global_device_ids=true | all-gather | bytes 294912 | tf_op jit(solution)/shard_map/all_gather | solution.py:19
  39.9 0.4 fusion.10
  40.3 10.0 %convolution_bitcast_fusion.1 = f32[1,16,3072]{2,1,0:T(8,128)S(1)} fusion(bf16[4096,3072]{1,0:T(8,128)(2,1)} %param.8, bf16[1,16,4096]{2,0,1:T(2,128)(2,1)S(1)} %get-tuple-element.5), kind=kOutput, calls=%fused_computation.2 | convolution fusion | flops 402653184 | bytes 25493504 | tf_op jit(solution)/shard_map/dot_general | solution.py:21
  50.2 10.0 %convolution_bitcast_fusion.2 = f32[1,16,3072]{2,1,0:T(8,128)S(1)} fusion(bf16[4096,3072]{1,0:T(8,128)(2,1)} %param.7, bf16[1,16,4096]{2,0,1:T(2,128)(2,1)S(1)} %get-tuple-element.5), kind=kOutput, calls=%fused_computation.3 | convolution fusion | flops 402653184 | bytes 25493504 | tf_op jit(solution)/shard_map/dot_general | solution.py:20
  60.2 11.5 %convolution_bitcast_fusion = f32[1,16,3072]{2,1,0:T(8,128)S(1)} fusion(bf16[3072,4096]{1,0:T(8,128)(2,1)} %param.9, bf16[1,16,4096]{2,0,1:T(2,128)(2,1)S(1)} %get-tuple-element.6), kind=kOutput, calls=%fused_computation.1 | convolution fusion | flops 402653184 | bytes 25493504 | tf_op jit(solution)/shard_map/dot_general | solution.py:22
  71.7 0.9 pad_maximum_fusion
  72.6 0.0 all-reduce.4.cloned.1.call-update
  72.6 0.0 all-reduce.6.cloned.1.call-start
  72.7 19.9 %all-reduce.4.cloned.1.call-done = f32[3,16,3072]{2,1,0:T(8,128)} async-done(((f32[3,16,3072]{2,1,0:T(8,128)}), f32[3,16,3072]{2,1,0:T(8,128)}) %all-reduce.4.cloned.1.call-update) | async-done | bytes 589840 | tf_op jit(solution)/shard_map/psum | solution.py:26
  92.6 0.0 copy-start
  92.6 14.9 %fusion.4 = f32[16,4096]{1,0:T(8,128)S(1)} fusion(bf16[4096,3072]{1,0:T(8,128)(2,1)} %param.7, f32[3,16,3072]{2,1,0:T(8,128)} %all-reduce.4.cloned.1.call-done), kind=kOutput, calls=%fused_computation.16 | convolution fusion | flops 403144704 | bytes 26017792 | tf_op jit(solution)/shard_map/dot_general | solution.py:28
  107.5 0.0 copy-done
  107.5 0.0 copy-start.2
  107.5 0.0 copy-start.1
  107.5 12.3 %convolution_add_fusion = f32[16,4096]{1,0:T(8,128)} fusion(f32[16,4096]{1,0:T(8,128)S(1)} %fusion.4, bf16[4096,3072]{1,0:T(8,128)(2,1)} %param.8, f32[3,16,3072]{2,1,0:T(8,128)S(1)} %copy-done), kind=kOutput, calls=%fused_computation | convolution fusion | flops 403013632 | bytes 26083328 | tf_op jit(solution)/shard_map/dot_general | solution.py:33
  119.8 0.0 all-reduce.6.cloned.1.call-update
  119.8 0.0 copy-done.2
  119.8 0.6 dynamic-slice
  121.1 70.6 %all-reduce.6.cloned.1.call-done = f32[16,4096]{1,0:T(8,128)} async-done(((f32[16,4096]{1,0:T(8,128)}), f32[16,4096]{1,0:T(8,128)}) %all-reduce.6.cloned.1.call-update) | async-done | bytes 262160
  191.7 0.0 copy-done.1
  191.7 1.5 dynamic-slice_multiply_fusion
  (1 shorter events, 0.0 us)
Async XLA Ops:
  6.5 86.1 %all-reduce.4.cloned.1.call-start = ((), (), s32[]{:S(2)}) async-start(), calls=%async_computation | async-start | bytes 1179648 | tf_op jit(solution)/shard_map/psum | solution.py:26
  72.6 119.1 %all-reduce.6.cloned.1.call-start = ((), (), s32[]{:S(2)}) async-start(), calls=%async_computation.1 | async-start | bytes 524288
  92.6 14.9 %copy-start = (f32[3,16,3072]{2,1,0:T(8,128)S(1)}, f32[3,16,3072]{2,1,0:T(8,128)}, u32[]{:S(2)}) copy-start(f32[3,16,3072]{2,1,0:T(8,128)} %all-reduce.4.cloned.1.call-done) | copy-start | bytes 1769476
  107.5 12.3 %copy-start.2 = (u32[32]{0:T(128)S(1)}, u32[32]{0:T(128)}, u32[]{:S(2)}) copy-start(u32[32]{0:T(128)} %constant.6) | copy-start | bytes 388
  107.5 84.2 %copy-start.1 = (bf16[2,4096]{1,0:T(2,128)(2,1)S(1)}, bf16[2,4096]{1,0:T(2,128)(2,1)}, u32[]{:S(2)}) copy-start(bf16[2,4096]{1,0:T(2,128)(2,1)} %param.5) | copy-start | bytes 49156
Sparse Core Ops, SparseCore 0:
  72.8 19.7 all-reduce.3
  119.9 71.7 all-reduce.5
where the time goes:
time: 200 us
  waiting for transfers between devices  90.6 us (45%)
  matrix products  58.6 us (29%)
  blocking collectives  32.5 us (16%)
  between operations  14.1 us (7%)
  other arithmetic  3.21 us (2%)
    unnamed x3, waiting for transfers between devices  70.7 us
    all_gather x1, blocking collectives, per_device(): piece = lax.all_gather(stacked, 'row', axis=1, tiled=True)  32.5 us
    psum x1, waiting for transfers between devices, per_device(): summed = lax.psum(partial_sums, 'col')  19.9 us
    dot_general x1, matrix products, per_device(): lax.dot_general(derived[0], w_gate, (((1,), (1,)), ((), ())), preferred_e...  14.9 us
    dot_general x1, matrix products, per_device(): lax.dot_general(derived[1], w_up, (((1,), (1,)), ((), ())), preferred_ele...  12.3 us
    dot_general x1, matrix products, per_device(): lax.dot_general(piece[1], w_down, (((1,), (1,)), ((), ())), preferred_ele...  11.5 us
    dot_general x1, matrix products, per_device(): gated = jnp.dot(piece[0], w_gate, preferred_element_type=jnp.float32)  9.97 us
    dot_general x1, matrix products, per_device(): upward = jnp.dot(piece[0], w_up, preferred_element_type=jnp.float32)  9.97 us
  transfers between devices with their start and end apart: 2, of which 2 were waited for; matrix products, arithmetic and copies ran while one was open for 0% of the time, Pallas kernels for 0%

commit v1 on v0

--- a/solution.py
+++ b/solution.py
@@ -16,7 +16,15 @@
 
 def per_device(inputs, out_grads, w_gate, w_up, w_down):
     stacked = jnp.stack([inputs, out_grads])
-    piece = lax.all_gather(stacked, "row", axis=1, tiled=True)
+    ways, here = (lax.axis_size("row"), lax.axis_index("row"))
+    grown, reach = (stacked, 1)
+    while reach < ways:
+        theirs = lax.ppermute(grown, "row", [(d, d ^ reach) for d in range(ways)])
+        mine_first = jnp.concatenate([grown, theirs], axis=1)
+        theirs_first = jnp.concatenate([theirs, grown], axis=1)
+        grown = jnp.where(here & reach == 0, mine_first, theirs_first)
+        reach = 2 * reach
+    piece = grown
     gated = jnp.dot(piece[0], w_gate, preferred_element_type=jnp.float32)
     upward = jnp.dot(piece[0], w_up, preferred_element_type=jnp.float32)
     backward = lax.dot_general(

time: 200 us -> 186 us (0.930)
  blocking collectives: 32.5 us -> 0 us
  waiting for transfers between devices: 90.6 us -> 99.6 us
  starting transfers between devices: 0.04 us -> 8.32 us
    all_gather x1 -> x0, blocking collectives: 32.5 us -> none  [per_device(): piece = lax.all_gather(stacked, 'row', axis=1, tiled=True)]
    ppermute x0 -> x3, starting transfers between devices: none -> 8.27 us  [per_device(): theirs = lax.ppermute(grown, 'row', [(d, d ^ reach) for d in range(ways)])]
    ppermute x0 -> x3, waiting for transfers between devices: none -> 7.1 us  [per_device(): theirs = lax.ppermute(grown, 'row', [(d, d ^ reach) for d in range(ways)])]
  transfers between devices with their start and end apart: 2 -> 5, of which waited for: 2 -> 5; matrix products, arithmetic and copies ran while one was open for 0% -> 0% of each run, Pallas kernels for 0% -> 0%
where the time goes in v1:
time: 186 us; the launch traced here: 185 us
  waiting for transfers between devices  99.6 us (54%)
  matrix products  58.4 us (31%)
  between operations  14.1 us (8%)
  starting transfers between devices  8.32 us (4%)
  other arithmetic  4.3 us (2%)
    unnamed x3, waiting for transfers between devices  70.7 us
    psum x1, waiting for transfers between devices, per_device(): summed = lax.psum(partial_sums, 'col')  21.8 us
    dot_general x1, matrix products, per_device(): lax.dot_general(derived[0], w_gate, (((1,), (1,)), ((), ())), preferred_e...  14.9 us
    dot_general x1, matrix products, per_device(): lax.dot_general(derived[1], w_up, (((1,), (1,)), ((), ())), preferred_ele...  12.3 us
    dot_general x1, matrix products, per_device(): lax.dot_general(piece[1], w_down, (((1,), (1,)), ((), ())), preferred_ele...  11.5 us
    dot_general x1, matrix products, per_device(): upward = jnp.dot(piece[0], w_up, preferred_element_type=jnp.float32)  9.89 us
    dot_general x1, matrix products, per_device(): gated = jnp.dot(piece[0], w_gate, preferred_element_type=jnp.float32)  9.89 us
    ppermute x3, starting transfers between devices, per_device(): theirs = lax.ppermute(grown, 'row', [(d, d ^ reach) for d in range(ways)])  8.27 us
  transfers between devices with their start and end apart: 5, of which 5 were waited for; matrix products, arithmetic and copies ran while one was open for 0% of the time, Pallas kernels for 0%

profile of v1, /device:TPU:0, one launch (start us, length us, event | category | flops | bytes accessed | tf_op | source)
XLA Modules:
  0.0 185.3 jit_solution(4549336296371238831)
XLA Ops:
  6.5 0.0 all-reduce.4.cloned.1.call-start
  6.5 0.8 pad_maximum_fusion.1
  7.3 3.0 %collective-permute-start = (bf16[2,2,4096]{2,1,0:T(2,128)(2,1)S(1)}, bf16[2,2,4096]{2,1,0:T(2,128)(2,1)S(1)}, u32[]{:S(2)}, u32[]{:S(2)}) collective-permute-start(bf16[2,2,4096]{2,1,0:T(2,128)(2,1)S(1)} %pad_maximum_fusion.1), channel_id=1, source_target_pairs={{0,2},{2,0},{4,6},{6,4},{8,10},{10,8},{12,14},{14,12},{1,3},{3,1},... | collective-permute-start | bytes 98312 | tf_op jit(solution)/shard_map/ppermute | solution.py:22
  10.3 1.9 %collective-permute-done = bf16[2,2,4096]{2,1,0:T(2,128)(2,1)S(1)} collective-permute-done((bf16[2,2,4096]{2,1,0:T(2,128)(2,1)S(1)}, bf16[2,2,4096]{2,1,0:T(2,128)(2,1)S(1)}, u32[]{:S(2)}, u32[]{:S(2)}) %collective-permute-start) | collective-permute-done | bytes 32800 | tf_op jit(solution)/shard_map/ppermute | solution.py:22
  12.2 0.9 maximum_select_fusion.2
  13.2 2.2 %collective-permute-start.1 = (bf16[2,4,4096]{2,1,0:T(4,128)(2,1)S(1)}, bf16[2,4,4096]{2,1,0:T(4,128)(2,1)S(1)}, u32[]{:S(2)}, u32[]{:S(2)}) collective-permute-start(bf16[2,4,4096]{2,1,0:T(4,128)(2,1)S(1)} %maximum_select_fusion.2), channel_id=1, source_target_pairs={{0,4},{2,6},{4,0},{6,2},{8,12},{10,14},{12,8},{14,10},{1,5},{3,7},... | collective-permute-start | bytes 196616 | tf_op jit(solution)/shard_map/ppermute | solution.py:22
  15.3 2.2 %collective-permute-done.1 = bf16[2,4,4096]{2,1,0:T(4,128)(2,1)S(1)} collective-permute-done((bf16[2,4,4096]{2,1,0:T(4,128)(2,1)S(1)}, bf16[2,4,4096]{2,1,0:T(4,128)(2,1)S(1)}, u32[]{:S(2)}, u32[]{:S(2)}) %collective-permute-start.1) | collective-permute-done | bytes 65568 | tf_op jit(solution)/shard_map/ppermute | solution.py:22
  17.6 0.1 maximum_select_fusion.1
  17.7 3.1 %collective-permute-start.2 = (bf16[2,8,4096]{2,1,0:T(8,128)(2,1)S(1)}, bf16[2,8,4096]{2,1,0:T(8,128)(2,1)S(1)}, u32[]{:S(2)}, u32[]{:S(2)}) collective-permute-start(bf16[2,8,4096]{2,1,0:T(8,128)(2,1)S(1)} %maximum_select_fusion.1), channel_id=1, source_target_pairs={{0,8},{2,10},{4,12},{6,14},{8,0},{10,2},{12,4},{14,6},{1,9},{3,11}... | collective-permute-start | bytes 393224 | tf_op jit(solution)/shard_map/ppermute | solution.py:22
  20.8 3.0 %collective-permute-done.2 = bf16[2,8,4096]{2,1,0:T(8,128)(2,1)S(1)} collective-permute-done((bf16[2,8,4096]{2,1,0:T(8,128)(2,1)S(1)}, bf16[2,8,4096]{2,1,0:T(8,128)(2,1)S(1)}, u32[]{:S(2)}, u32[]{:S(2)}) %collective-permute-start.2) | collective-permute-done | bytes 131104 | tf_op jit(solution)/shard_map/ppermute | solution.py:22
  23.8 11.5 %convolution_bitcast_fusion = f32[1,16,3072]{2,1,0:T(8,128)S(1)} fusion(bf16[3072,4096]{1,0:T(8,128)(2,1)} %param.9, bf16[2,16,4096]{2,1,0:T(8,128)(2,1)S(1)} %maximum_select_fusion), kind=kOutput, calls=%fused_computation.1 | convolution fusion | flops 402653184 | bytes 25493504 | tf_op jit(solution)/shard_map/dot_general | solution.py:30
  35.3 9.9 %convolution_bitcast_fusion.1 = f32[1,16,3072]{2,1,0:T(8,128)S(1)} fusion(bf16[4096,3072]{1,0:T(8,128)(2,1)} %param.8, bf16[2,16,4096]{2,1,0:T(8,128)(2,1)S(1)} %maximum_select_fusion), kind=kOutput, calls=%fused_computation.2 | convolution fusion | flops 402653184 | bytes 25493504 | tf_op jit(solution)/shard_map/dot_general | solution.py:29
  45.2 9.9 %convolution_bitcast_fusion.2 = f32[1,16,3072]{2,1,0:T(8,128)S(1)} fusion(bf16[4096,3072]{1,0:T(8,128)(2,1)} %param.7, bf16[2,16,4096]{2,1,0:T(8,128)(2,1)S(1)} %maximum_select_fusion), kind=kOutput, calls=%fused_computation.3 | convolution fusion | flops 402653184 | bytes 25493504 | tf_op jit(solution)/shard_map/dot_general | solution.py:28
  55.1 0.9 pad_maximum_fusion
  56.0 0.0 all-reduce.4.cloned.1.call-update
  56.0 0.0 all-reduce.6.cloned.1.call-start
  56.1 21.8 %all-reduce.4.cloned.1.call-done = f32[3,16,3072]{2,1,0:T(8,128)} async-done(((f32[3,16,3072]{2,1,0:T(8,128)}), f32[3,16,3072]{2,1,0:T(8,128)}) %all-reduce.4.cloned.1.call-update) | async-done | bytes 589840 | tf_op jit(solution)/shard_map/psum | solution.py:34
  77.9 0.0 copy-start
  77.9 14.9 %fusion.4 = f32[16,4096]{1,0:T(8,128)S(1)} fusion(bf16[4096,3072]{1,0:T(8,128)(2,1)} %param.7, f32[3,16,3072]{2,1,0:T(8,128)} %all-reduce.4.cloned.1.call-done), kind=kOutput, calls=%fused_computation.18 | convolution fusion | flops 403144704 | bytes 26017792 | tf_op jit(solution)/shard_map/dot_general | solution.py:36
  92.8 0.0 copy-done
  92.8 0.0 copy-start.2
  92.8 0.0 copy-start.1
  92.8 12.3 %convolution_add_fusion = f32[16,4096]{1,0:T(8,128)} fusion(f32[16,4096]{1,0:T(8,128)S(1)} %fusion.4, bf16[4096,3072]{1,0:T(8,128)(2,1)} %param.8, f32[3,16,3072]{2,1,0:T(8,128)S(1)} %copy-done), kind=kOutput, calls=%fused_computation | convolution fusion | flops 403013632 | bytes 26083328 | tf_op jit(solution)/shard_map/dot_general | solution.py:41
  105.0 0.0 all-reduce.6.cloned.1.call-update
  105.1 0.0 copy-done.2
  105.1 0.6 dynamic-slice
  106.3 70.6 %all-reduce.6.cloned.1.call-done = f32[16,4096]{1,0:T(8,128)} async-done(((f32[16,4096]{1,0:T(8,128)}), f32[16,4096]{1,0:T(8,128)}) %all-reduce.6.cloned.1.call-update) | async-done | bytes 262160
  177.0 0.0 copy-done.1
  177.0 1.5 dynamic-slice_multiply_fusion
  (1 shorter events, 0.0 us)
Async XLA Ops:
  6.5 71.3 %all-reduce.4.cloned.1.call-start = ((), (), s32[]{:S(2)}) async-start(), calls=%async_computation | async-start | bytes 1179648 | tf_op jit(solution)/shard_map/psum | solution.py:34
  7.3 4.9 %collective-permute-start = (bf16[2,2,4096]{2,1,0:T(2,128)(2,1)S(1)}, bf16[2,2,4096]{2,1,0:T(2,128)(2,1)S(1)}, u32[]{:S(2)}, u32[]{:S(2)}) collective-permute-start(bf16[2,2,4096]{2,1,0:T(2,128)(2,1)S(1)} %pad_maximum_fusion.1), channel_id=1, source_target_pairs={{0,2},{2,0},{4,6},{6,4},{8,10},{10,8},{12,14},{14,12},{1,3},{3,1},... | collective-permute-start | bytes 98312 | tf_op jit(solution)/shard_map/ppermute | solution.py:22
  13.2 4.4 %collective-permute-start.1 = (bf16[2,4,4096]{2,1,0:T(4,128)(2,1)S(1)}, bf16[2,4,4096]{2,1,0:T(4,128)(2,1)S(1)}, u32[]{:S(2)}, u32[]{:S(2)}) collective-permute-start(bf16[2,4,4096]{2,1,0:T(4,128)(2,1)S(1)} %maximum_select_fusion.2), channel_id=1, source_target_pairs={{0,4},{2,6},{4,0},{6,2},{8,12},{10,14},{12,8},{14,10},{1,5},{3,7},... | collective-permute-start | bytes 196616 | tf_op jit(solution)/shard_map/ppermute | solution.py:22
  17.7 6.1 %collective-permute-start.2 = (bf16[2,8,4096]{2,1,0:T(8,128)(2,1)S(1)}, bf16[2,8,4096]{2,1,0:T(8,128)(2,1)S(1)}, u32[]{:S(2)}, u32[]{:S(2)}) collective-permute-start(bf16[2,8,4096]{2,1,0:T(8,128)(2,1)S(1)} %maximum_select_fusion.1), channel_id=1, source_target_pairs={{0,8},{2,10},{4,12},{6,14},{8,0},{10,2},{12,4},{14,6},{1,9},{3,11}... | collective-permute-start | bytes 393224 | tf_op jit(solution)/shard_map/ppermute | solution.py:22
  56.0 121.0 %all-reduce.6.cloned.1.call-start = ((), (), s32[]{:S(2)}) async-start(), calls=%async_computation.1 | async-start | bytes 524288
  77.9 14.9 %copy-start = (f32[3,16,3072]{2,1,0:T(8,128)S(1)}, f32[3,16,3072]{2,1,0:T(8,128)}, u32[]{:S(2)}) copy-start(f32[3,16,3072]{2,1,0:T(8,128)} %all-reduce.4.cloned.1.call-done) | copy-start | bytes 1769476
  92.8 12.3 %copy-start.2 = (u32[32]{0:T(128)S(1)}, u32[32]{0:T(128)}, u32[]{:S(2)}) copy-start(u32[32]{0:T(128)} %constant.20) | copy-start | bytes 388
  92.8 84.2 %copy-start.1 = (bf16[2,4096]{1,0:T(2,128)(2,1)S(1)}, bf16[2,4096]{1,0:T(2,128)(2,1)}, u32[]{:S(2)}) copy-start(bf16[2,4096]{1,0:T(2,128)(2,1)} %param.5) | copy-start | bytes 49156
Sparse Core Ops, SparseCore 0:
  56.1 21.6 all-reduce.3
  105.2 71.7 all-reduce.5

commit v2 on v0

--- a/solution.py
+++ b/solution.py
@@ -23,7 +23,7 @@
         piece[1], w_down, (((1,), (1,)), ((), ())), preferred_element_type=jnp.float32
     )
     partial_sums = jnp.stack([gated, upward, backward])
-    summed = lax.psum(partial_sums, "col")
+    summed = jnp.sum(lax.all_gather(partial_sums, "col"), axis=0)
     derived = derivatives(summed)
     total = lax.dot_general(
         derived[0], w_gate, (((1,), (1,)), ((), ())), preferred_element_type=jnp.float32

time: 200 us -> 189 us (0.945)
  waiting for transfers between devices: 90.6 us -> 81 us
  matrix products: 58.6 us -> 55.2 us
    psum x1 -> x0, waiting for transfers between devices: 19.9 us -> none  [per_device(): summed = lax.psum(partial_sums, 'col')]
    all_gather x0 -> x1, waiting for transfers between devices: none -> 10.3 us  [per_device(): summed = jnp.sum(lax.all_gather(partial_sums, 'col'), axis=0)]
    dot_general x1, matrix products: 14.9 us -> 11.5 us  [per_device(): lax.dot_general(derived[0], w_gate, (((1,), (1,)), ((), ())), preferred_e...]
where the time goes in v2:
time: 189 us
  waiting for transfers between devices  81 us (43%)
  matrix products  55.2 us (29%)
  blocking collectives  32.5 us (17%)
  between operations  14.1 us (7%)
  other arithmetic  4.63 us (2%)
    unnamed x3, waiting for transfers between devices  70.7 us
    all_gather x1, blocking collectives, per_device(): piece = lax.all_gather(stacked, 'row', axis=1, tiled=True)  32.5 us
    dot_general x1, matrix products, per_device(): lax.dot_general(derived[1], w_up, (((1,), (1,)), ((), ())), preferred_ele...  12.3 us
    dot_general x1, matrix products, per_device(): lax.dot_general(piece[1], w_down, (((1,), (1,)), ((), ())), preferred_ele...  11.5 us
    dot_general x1, matrix products, per_device(): lax.dot_general(derived[0], w_gate, (((1,), (1,)), ((), ())), preferred_e...  11.5 us
    all_gather x1, waiting for transfers between devices, per_device(): summed = jnp.sum(lax.all_gather(partial_sums, 'col'), axis=0)  10.3 us
    dot_general x1, matrix products, per_device(): gated = jnp.dot(piece[0], w_gate, preferred_element_type=jnp.float32)  9.97 us
    dot_general x1, matrix products, per_device(): upward = jnp.dot(piece[0], w_up, preferred_element_type=jnp.float32)  9.97 us
  transfers between devices with their start and end apart: 2, of which 2 were waited for; matrix products, arithmetic and copies ran while one was open for 0% of the time, Pallas kernels for 0%

profile of v2, /device:TPU:0, one launch (start us, length us, event | category | flops | bytes accessed | tf_op | source)
XLA Modules:
  0.0 188.5 jit_solution(10522026716130323047)
XLA Ops:
  6.5 0.0 all-gather.3.cloned.1.call-start
  6.5 0.8 pad_maximum_fusion.1
  7.4 32.5 %all_gather.9 = bf16[2,16,4096]{2,0,1:T(2,128)(2,1)S(1)} all-gather(bf16[2,2,4096]{2,0,1:T(2,128)(2,1)S(1)} %copy.6), channel_id=1, replica_groups=mesh['groups'=2,'row'=8,'col'=2] {'row'}, dimensions={1}, use_global_device_ids=true | all-gather | bytes 294912 | tf_op jit(solution)/shard_map/all_gather | solution.py:19
  39.9 0.4 fusion.10
  40.3 10.0 %convolution_bitcast_fusion.1 = f32[1,16,3072]{2,1,0:T(8,128)S(1)} fusion(bf16[4096,3072]{1,0:T(8,128)(2,1)} %param.8, bf16[1,16,4096]{2,0,1:T(2,128)(2,1)S(1)} %get-tuple-element.5), kind=kOutput, calls=%fused_computation.2 | convolution fusion | flops 402653184 | bytes 25493504 | tf_op jit(solution)/shard_map/dot_general | solution.py:21
  50.2 10.0 %convolution_bitcast_fusion.2 = f32[1,16,3072]{2,1,0:T(8,128)S(1)} fusion(bf16[4096,3072]{1,0:T(8,128)(2,1)} %param.7, bf16[1,16,4096]{2,0,1:T(2,128)(2,1)S(1)} %get-tuple-element.5), kind=kOutput, calls=%fused_computation.3 | convolution fusion | flops 402653184 | bytes 25493504 | tf_op jit(solution)/shard_map/dot_general | solution.py:20
  60.2 11.5 %convolution_bitcast_fusion = f32[1,16,3072]{2,1,0:T(8,128)S(1)} fusion(bf16[3072,4096]{1,0:T(8,128)(2,1)} %param.9, bf16[1,16,4096]{2,0,1:T(2,128)(2,1)S(1)} %get-tuple-element.6), kind=kOutput, calls=%fused_computation.1 | convolution fusion | flops 402653184 | bytes 25493504 | tf_op jit(solution)/shard_map/dot_general | solution.py:22
  71.7 0.9 pad_maximum_fusion
  72.6 0.0 all-gather.3.cloned.1.call-update
  72.7 0.0 all-reduce.3.cloned.1.call-start
  72.7 10.3 %all-gather.3.cloned.1.call-done = f32[6,16,3072]{2,1,0:T(8,128)} async-done(((f32[3,16,3072]{2,1,0:T(8,128)}), f32[6,16,3072]{2,1,0:T(8,128)}) %all-gather.3.cloned.1.call-update) | async-done | bytes 1179664 | tf_op jit(solution)/shard_map/all_gather | solution.py:26
  83.0 1.4 reduce_sum.9
  84.4 11.5 %fusion.4 = f32[16,4096]{1,0:T(8,128)S(1)} fusion(bf16[4096,3072]{1,0:T(8,128)(2,1)} %param.7, f32[3,16,3072]{2,1,0:T(8,128)S(1)} %reduce_sum.9), kind=kOutput, calls=%fused_computation.16 | convolution fusion | flops 403144704 | bytes 26017792 | tf_op jit(solution)/shard_map/dot_general | solution.py:28
  95.9 0.0 copy-start.1
  95.9 0.0 copy-start
  95.9 12.3 %convolution_add_fusion = f32[16,4096]{1,0:T(8,128)} fusion(f32[16,4096]{1,0:T(8,128)S(1)} %fusion.4, bf16[4096,3072]{1,0:T(8,128)(2,1)} %param.8, f32[3,16,3072]{2,1,0:T(8,128)S(1)} %reduce_sum.9), kind=kOutput, calls=%fused_computation | convolution fusion | flops 403013632 | bytes 26083328 | tf_op jit(solution)/shard_map/dot_general | solution.py:33
  108.2 0.0 all-reduce.3.cloned.1.call-update
  108.2 0.0 copy-done.1
  108.2 0.6 dynamic-slice
  109.5 70.7 %all-reduce.3.cloned.1.call-done = f32[16,4096]{1,0:T(8,128)} async-done(((f32[16,4096]{1,0:T(8,128)}), f32[16,4096]{1,0:T(8,128)}) %all-reduce.3.cloned.1.call-update) | async-done | bytes 262160
  180.1 0.0 copy-done
  180.1 1.5 dynamic-slice_multiply_fusion
  (1 shorter events, 0.0 us)
Async XLA Ops:
  6.5 76.5 %all-gather.3.cloned.1.call-start = ((), (), s32[]{:S(2)}) async-start(), calls=%async_computation | async-start | bytes 1769472 | tf_op jit(solution)/shard_map/all_gather | solution.py:26
  72.7 107.5 %all-reduce.3.cloned.1.call-start = ((), (), s32[]{:S(2)}) async-start(), calls=%async_computation.1 | async-start | bytes 524288
  95.9 12.3 %copy-start.1 = (u32[32]{0:T(128)S(1)}, u32[32]{0:T(128)}, u32[]{:S(2)}) copy-start(u32[32]{0:T(128)} %constant.8) | copy-start | bytes 388
  95.9 84.2 %copy-start = (bf16[2,4096]{1,0:T(2,128)(2,1)S(1)}, bf16[2,4096]{1,0:T(2,128)(2,1)}, u32[]{:S(2)}) copy-start(bf16[2,4096]{1,0:T(2,128)(2,1)} %param.5) | copy-start | bytes 49156
Sparse Core Ops, SparseCore 0:
  72.8 10.1 all-gather.2
  108.3 71.7 all-reduce.2
